TPU v7x, 32 devices: a whole 2x2x4 slice. The times are simulated.
32 devices in a mesh: req: 8 (over z, x), cfg: 2 (over core), seq: 2 (over y).
Axes of the slice: x: 2, y: 2, z: 4, core: 2. Of those that a mesh axis runs over, the one named last changes fastest.
Arguments:
- queries: bfloat16 [8, 2, 512, 1024], P('req', 'cfg', 'seq'), may hold values from -48 to 48
- key_vectors: bfloat16 [8, 2, 512, 1024], P('req', 'cfg', 'seq'), may hold values from -48 to 48
- values: bfloat16 [8, 2, 512, 1024], P('req', 'cfg', 'seq'), may hold values from -6 to 6
- hidden: bfloat16 [8, 2, 512, 1536], P('req', 'cfg', 'seq'), may hold values from -15 to 15
- out_proj: bfloat16 [1024, 1536], P('req'), may hold values from -0.1875 to 0.1875
- head_weight: bfloat16 [1536, 64], replicated, may hold values from -0.15625 to 0.15625
- head_bias: float32 [64], replicated, may hold values from -3 to 3
- attn_gate: float32 [8, 1536], P('req'), may hold values from 0.5 to 4
- shift_scale: float32 [8, 2, 1536], P('req'), may hold values from -3 to 3
- grid_shape: int32 [8, 3], P('req'), may hold values from 1 to 32, as said below
- step_index: int32 [8], P('req'), may hold values from 0 to 19
- guide_scale: float32 [8], P('req'), may hold values from 3 to 6
- latent: float32 [8, 512, 64], P('req', 'seq', 'cfg'), may hold values from -6 to 6
Outputs:
- next_latent: float32 [8, 512, 64], P('req', 'seq', 'cfg')
- velocity: float32 [8, 512, 64], P('req', 'seq', 'cfg')
Inputs may be any that keep to these rules, and one draw needn't show every extreme that they name: `grid_shape`: the frames are at most 2, the height at most 8 and the width at most 32, so that frames * height * width is at most 512; in every draw some request fills all 512 slots.
All inputs are finite; a program needn't handle non-finite values.
Results may differ from a plain program's by a relative error of at most 0.0052.
Values may be sent and summed in bfloat16 or wider, within the bound.
A program may use at most 64 MiB of HBM per device.

v0:
```python
import math
import jax
import jax.numpy as jnp
from jax import lax
from jax.sharding import PartitionSpec as P

HEAD_DIM = 128
STEPS = 20
masked_score = -1e30
norm_eps = 1e-06
shift_factor = 5.0


def partner_2(block, axis, distance):
    count = lax.axis_size(axis)
    route = []
    for low in range(count):
        high = low | 1 << distance
        if high != low and high < count:
            route += [(low, high), (high, low)]
    return lax.ppermute(block, axis, route)


def rotary(vectors, grid_dims, first_token):
    row_count, col_count = vectors.shape
    sixth_dim = HEAD_DIM // 6
    time_pairs = (HEAD_DIM - 4 * sixth_dim) // 2
    column = jnp.arange(col_count, dtype=jnp.int32) % HEAD_DIM
    pair_index = column // 2
    space_pair = (pair_index - time_pairs).astype(jnp.float32)
    is_time = pair_index < time_pairs
    is_height = jnp.logical_and(pair_index >= time_pairs, pair_index < time_pairs + sixth_dim)
    exponent = jnp.where(
        is_time,
        pair_index.astype(jnp.float32) / time_pairs,
        jnp.where(is_height, space_pair / sixth_dim, (space_pair - sixth_dim) / sixth_dim),
    )
    frequency = jnp.power(jnp.float32(10000.0), -exponent)
    token_ids = first_token + jnp.arange(row_count, dtype=jnp.int32)
    plane_size = grid_dims[1] * grid_dims[2]
    frame_ids = token_ids // plane_size
    height = token_ids // grid_dims[2] % grid_dims[1]
    across = token_ids % grid_dims[2]
    position = jnp.where(
        is_time[None, :],
        frame_ids[:, None],
        jnp.where(is_height[None, :], height[:, None], across[:, None]),
    ).astype(jnp.float32)
    angles = position * frequency[None, :]
    is_even = column % 2 == 0
    source = vectors.astype(jnp.float32)
    partner = jnp.where(is_even[None, :], jnp.roll(source, -1, axis=1), jnp.roll(source, 1, axis=1))
    sign_flip = jnp.where(is_even, -1.0, 1.0).astype(jnp.float32)
    turned = source * jnp.cos(angles) + partner * (jnp.sin(angles) * sign_flip[None, :])
    return turned.astype(jnp.bfloat16)


def noise_level(step_value):
    progress = 1.0 - step_value.astype(jnp.float32) / STEPS
    return shift_factor * progress / (1.0 + (shift_factor - 1.0) * progress)


def output_head(hidden_rows, proj, gate_row, modulation, head_weight, head_bias):
    mixed_rows = hidden_rows.astype(jnp.float32) + gate_row[None, :] * proj
    average = jnp.mean(mixed_rows, axis=-1, keepdims=True)
    centered = mixed_rows - average
    spread = jnp.mean(centered * centered, axis=-1, keepdims=True)
    normed = centered * lax.rsqrt(spread + norm_eps)
    modded = (normed * (1.0 + modulation[1][None, :]) + modulation[0][None, :]).astype(jnp.bfloat16)
    return jnp.dot(modded, head_weight, preferred_element_type=jnp.float32) + head_bias[None, :]


def attend_all(query_heads, key_heads, value_heads, length):
    total_rows = query_heads.shape[0]
    block_rows = min(512, total_rows)
    score_scale = 1.0 / math.sqrt(HEAD_DIM)
    live_keys = jnp.arange(total_rows, dtype=jnp.int32) < length

    def one_block(start):
        query_block = lax.dynamic_slice_in_dim(query_heads, start, block_rows, 0)
        scores = (
            jnp.einsum("qhd,khd->hqk", query_block, key_heads, preferred_element_type=jnp.float32)
            * score_scale
        )
        scores = jnp.where(live_keys[None, None, :], scores, masked_score)
        row_max = jnp.max(scores, axis=-1, keepdims=True)
        exponent = jnp.exp(scores - row_max)
        row_sum = jnp.sum(exponent, axis=-1, keepdims=True)
        weights = (exponent / row_sum).astype(jnp.bfloat16)
        output = jnp.einsum(
            "hqk,khd->qhd", weights, value_heads, preferred_element_type=jnp.float32
        )
        return output.astype(jnp.bfloat16)

    starts = jnp.arange(total_rows // block_rows, dtype=jnp.int32) * block_rows
    return lax.map(one_block, starts).reshape(total_rows, -1)


def on_device(
    queries,
    key_vectors,
    values,
    hidden,
    out_proj,
    head_weight,
    head_bias,
    attn_gate,
    shift_scale,
    grid_shape,
    step_index,
    guide_scale,
    latent,
):
    row_count = queries.shape[2]
    grid_dims = grid_shape[0]
    length = grid_dims[0] * grid_dims[1] * grid_dims[2]
    first_token = lax.axis_index("seq") * row_count
    rot_q = rotary(queries[0, 0], grid_dims, first_token)
    rot_k = rotary(key_vectors[0, 0], grid_dims, first_token)
    head_q, head_k, head_v = (
        lax.all_to_all(rot_q, "seq", split_axis=1, concat_axis=0, tiled=True),
        lax.all_to_all(rot_k, "seq", split_axis=1, concat_axis=0, tiled=True),
        lax.all_to_all(values[0, 0], "seq", split_axis=1, concat_axis=0, tiled=True),
    )
    total_rows = head_q.shape[0]
    local_heads = head_q.shape[1] // HEAD_DIM
    head_shape = (total_rows, local_heads, HEAD_DIM)
    query_heads = head_q.reshape(head_shape)
    key_heads = head_k.reshape(head_shape)
    value_heads = head_v.reshape(head_shape)
    head_result = attend_all(query_heads, key_heads, value_heads, length)
    attended = lax.all_to_all(head_result, "seq", split_axis=0, concat_axis=1, tiled=True)
    proj = jnp.dot(
        attended,
        lax.all_gather(out_proj, "req", axis=0, tiled=True),
        preferred_element_type=jnp.float32,
    )
    prediction = output_head(
        hidden[0, 0], proj, attn_gate[0], shift_scale[0], head_weight, head_bias
    )
    own_width = latent.shape[2]
    cfg_place = lax.axis_index("cfg")
    own_cols = lax.dynamic_slice_in_dim(prediction, cfg_place * own_width, own_width, 1)
    partner_cols = lax.dynamic_slice_in_dim(prediction, (1 - cfg_place) * own_width, own_width, 1)
    other_half = partner_2(partner_cols, "cfg", 0)
    is_cond = cfg_place == 0
    cond_pred = jnp.where(is_cond, own_cols, other_half)
    uncond_pred = jnp.where(is_cond, other_half, own_cols)
    guided = uncond_pred + guide_scale[0] * (cond_pred - uncond_pred)
    live_rows = first_token + jnp.arange(row_count, dtype=jnp.int32) < length
    velocity = jnp.where(live_rows[:, None], guided, jnp.float32(0.0))
    delta_level = noise_level(step_index[0] + 1) - noise_level(step_index[0])
    next_latent = latent[0] + delta_level * velocity
    return (next_latent[None], velocity[None])


def solution(mesh):
    return jax.shard_map(
        on_device,
        mesh=mesh,
        in_specs=(
            P("req", "cfg", "seq", None),
            P("req", "cfg", "seq", None),
            P("req", "cfg", "seq", None),
            P("req", "cfg", "seq", None),
            P("req", None),
            P(),
            P(),
            P("req", None),
            P("req", None, None),
            P("req", None),
            P("req"),
            P("req"),
            P("req", "seq", "cfg"),
        ),
        out_specs=(P("req", "seq", "cfg"), P("req", "seq", "cfg")),
        check_vma=False,
    )
```

profile of v0, /device:TPU:1, one launch (start us, length us, event | category | flops | bytes accessed | tf_op | source)
XLA Modules:
  0.0 87.9 jit_solution(608926784474118634)
XLA Ops:
  7.2 0.0 copy-start
  7.2 0.0 copy-start.1
  7.2 0.0 all-gather.2.cloned.1.call-start
  7.2 0.7 all-gather.2.cloned.1.call-update
  7.9 1.4 %fusion.34 = (s32[1,1]{1,0:T(1,128)}, s32[1,1]{1,0:T(1,128)}, s32[1,1]{1,0:T(1,128)}) fusion(s32[1,3]{1,0:T(1,128)} %param.22), kind=kLoop, calls=%fused_computation.78 | loop fusion | bytes 24 | tf_op jit(solution)/shard_map/slice | solution.py:116
  14.0 2.1 %reshape.291 = f32[256,2,512]{2,1,0:T(2,128)S(1)} reshape(bf16[1,1,256,1024]{3,2,1,0:T(8,128)(2,1)} %param.13) | data formatting | bytes 1572864 | tf_op jit(solution)/shard_map/convert_element_type | solution.py:51
  16.1 2.1 %reshape.293 = f32[256,2,512]{2,1,0:T(2,128)S(1)} reshape(bf16[1,1,256,1024]{3,2,1,0:T(8,128)(2,1)} %param.14) | data formatting | bytes 1572864 | tf_op jit(solution)/shard_map/convert_element_type | solution.py:51
  18.1 0.1 and_select_fusion.6
  18.3 0.9 %and_select_fusion.3 = (s32[256]{0:T(256)S(1)}, s32[256]{0:T(256)S(1)}) fusion(pred[]{:T(512)S(6)} %lt.119, s32[]{:T(128)S(6)} %select_n.201, s32[]{:T(128)S(6)} %mul.133, pred[]{:T(512)S(6)} %lt.117, s32[]{:T(128)S(6)} %select_n.199, s32[]{:T(128)} %bitcast.4, s32[]{:T(128)S(6)} %sign.48), kind=kLoop, calls=%fused_computation.61 | loop fusion | flops 5888 | bytes 2070 | tf_op jit(solution)/shard_map/jit(remainder)/select_n | solution.py:43
  19.3 0.0 copy-done.1
  19.3 0.1 convert_bitcast_fusion
  19.4 0.1 fusion.33
  19.5 0.4 fusion.32
  19.9 0.0 copy-start.2
  19.9 0.4 pad_maximum_fusion.2
  20.4 0.6 copy-done.2
  21.0 0.1 convert_bitcast_fusion.1
  21.1 0.1 fusion.31
  21.2 0.4 fusion.30
  21.6 0.4 pad_maximum_fusion
  22.0 0.0 copy-start.3
  22.1 5.4 %fusion.14 = (bf16[256,2,512]{2,0,1:T(8,128)(2,1)S(1)}, bf16[256,2,512]{2,0,1:T(8,128)(2,1)}) fusion(f32[32,2,8,512]{3,2,1,0:T(8,128)S(1)} %bitcast.64, f32[32,2,8,512]{3,2,1,0:T(8,128)S(1)} %bitcast.63, f32[256,2,512]{2,1,0:T(2,128)S(1)} %reshape.291, f32[2,512]{1,0:T(2,128)S(1)} %get-tuple-element.50, f32[2,512]{1,0:T(2,128)S(1)} %get-tuple-element.49, ...), kind=kLoop, calls=%fused_computation.23 | loop fusion | flops 3932160 | bytes 7354368 | tf_op jit(solution)/shard_map/convert_element_type | solution.py:55
  27.5 10.2 %all_to_all.61 = bf16[256,2,512]{2,0,1:T(8,128)(2,1)S(1)} all-to-all(bf16[256,2,512]{2,0,1:T(8,128)(2,1)S(1)} %get-tuple-element.32), channel_id=1, replica_groups=mesh['req'=8,'cfg'=2,'seq'=2] {'seq'}, dimensions={1} | all-to-all | bytes 1048576 | tf_op jit(solution)/shard_map/all_to_all | solution.py:121
  37.7 3.5 %all-to-all-start.1 = ((bf16[256,2,512]{2,0,1:T(8,128)(2,1)}), bf16[256,2,512]{2,0,1:T(8,128)(2,1)S(1)}, u32[]{:S(2)}, u32[]{:S(2)}) async-start(bf16[256,2,512]{2,0,1:T(8,128)(2,1)} %get-tuple-element.33), calls=%async_computation.1 | async-start | bytes 1048576 | tf_op jit(solution)/shard_map/all_to_all | solution.py:122
  41.2 0.0 copy-done.3
  41.2 0.4 all_to_all.50
  41.5 0.9 copy.24
  42.4 5.0 %all-to-all-done.1 = bf16[256,2,512]{2,0,1:T(8,128)(2,1)S(1)} async-done(((bf16[256,2,512]{2,0,1:T(8,128)(2,1)}), bf16[256,2,512]{2,0,1:T(8,128)(2,1)S(1)}, u32[]{:S(2)}, u32[]{:S(2)}) %all-to-all-start.1) | async-done | bytes 524320 | tf_op jit(solution)/shard_map/all_to_all | solution.py:122
  47.4 3.5 %all-to-all-start.2 = ((bf16[256,2,512]{2,0,1:T(8,128)(2,1)}), bf16[256,2,512]{2,0,1:T(8,128)(2,1)S(1)}, u32[]{:S(2)}, u32[]{:S(2)}) async-start(bf16[256,2,512]{2,0,1:T(8,128)(2,1)} %copy.24), calls=%async_computation.2 | async-start | bytes 1048576 | tf_op jit(solution)/shard_map/all_to_all | solution.py:123
  52.9 0.1 reshape.281
  53.0 0.1 reshape.282
  53.1 3.6 %all-to-all-done.2 = bf16[256,2,512]{2,0,1:T(8,128)(2,1)S(1)} async-done(((bf16[256,2,512]{2,0,1:T(8,128)(2,1)}), bf16[256,2,512]{2,0,1:T(8,128)(2,1)S(1)}, u32[]{:S(2)}, u32[]{:S(2)}) %all-to-all-start.2) | async-done | bytes 524320 | tf_op jit(solution)/shard_map/all_to_all | solution.py:123
  56.7 0.1 reshape.283
  56.8 0.7 fusion.20
  57.5 1.4 %fusion.35 = (f32[4,512]{1,0:T(4,128)S(1)}, f32[4,512,512]{1,2,0:T(8,128)S(1)}) fusion(f32[4,512,512]{1,2,0:T(8,128)S(1)} %fusion.20, pred[512]{0:T(512)(128)(4,1)S(1)} %iota_compare_fusion), kind=kOutput, calls=%fused_computation.79 | output fusion | flops 6291967 | bytes 8397312 | tf_op jit(solution)/shard_map/while/body/eval_jaxpr/sub | solution.py:87
  59.0 0.9 %fusion.8 = bf16[512,4,128]{2,0,1:T(8,128)(2,1)S(1)} fusion(f32[4,512,512]{1,2,0:T(8,128)S(1)} %get-tuple-element.38, f32[4,512]{1,0:T(4,128)S(1)} %get-tuple-element.37, bf16[512,4,128]{2,1,0:T(4,128)(2,1)S(1)} %reshape.283), kind=kOutput, calls=%fused_computation.14 | convolution fusion | flops 270794752 | bytes 5251072 | tf_op jit(solution)/shard_map/while/body/eval_jaxpr/hqk,khd->qhd/dot_general | solution.py:90
  59.9 0.0 copy-start.6
  59.9 0.0 copy-start.5
  59.9 0.0 copy-start.7
  59.9 0.4 copy.27
  60.3 1.0 %all_to_all.53 = bf16[2,256,512]{2,1,0:T(8,128)(2,1)} reshape(bf16[512,4,128]{2,1,0:T(4,128)(2,1)S(1)} %copy.27) | data formatting | bytes 1048576 | tf_op jit(solution)/shard_map/all_to_all | solution.py:132
  61.3 3.5 %all-to-all-start.3 = ((bf16[2,256,512]{2,1,0:T(8,128)(2,1)}), bf16[2,256,512]{2,1,0:T(8,128)(2,1)S(1)}, u32[]{:S(2)}, u32[]{:S(2)}) async-start(bf16[2,256,512]{2,1,0:T(8,128)(2,1)} %all_to_all.53), calls=%async_computation.3 | async-start | bytes 1048576 | tf_op jit(solution)/shard_map/all_to_all | solution.py:132
  64.8 0.0 copy-done.6
  64.9 0.0 copy-done.5
  64.9 5.7 %all-to-all-done.3 = bf16[2,256,512]{2,1,0:T(8,128)(2,1)S(1)} async-done(((bf16[2,256,512]{2,1,0:T(8,128)(2,1)}), bf16[2,256,512]{2,1,0:T(8,128)(2,1)S(1)}, u32[]{:S(2)}, u32[]{:S(2)}) %all-to-all-start.3) | async-done | bytes 524320 | tf_op jit(solution)/shard_map/all_to_all | solution.py:132
  70.7 0.2 copy.28
  70.9 1.1 %all-gather.2.cloned.1.call-done = bf16[1024,1536]{1,0:T(8,128)(2,1)} async-done(((bf16[128,1536]{1,0:T(8,128)(2,1)}), bf16[1024,1536]{1,0:T(8,128)(2,1)}) %all-gather.2.cloned.1.call-update) | async-done | bytes 3145744 | tf_op jit(solution)/shard_map/all_gather | solution.py:135
  71.9 0.0 copy-done.7
  71.9 0.0 copy-start.8
  71.9 3.0 %fusion.36 = (f32[256]{0:T(256)S(1)}, f32[256,1536]{1,0:T(8,128)S(1)}) fusion(bf16[256,1024]{0,1:T(8,128)(2,1)S(1)} %bitcast.69, bf16[1024,1536]{1,0:T(8,128)(2,1)} %all-gather.2.cloned.1.call-done, f32[1536]{0:T(1024)S(1)} %reduce, bf16[1,1,256,1536]{3,2,1,0:T(8,128)(2,1)S(1)} %copy-done.7), kind=kOutput, calls=%fused_computation.80 | convolution fusion | flops 806878976 | bytes 6036480 | tf_op jit(solution)/shard_map/dot_general | solution.py:133
  74.9 0.0 copy-start.4
  74.9 0.3 multiply_reduce_fusion
  75.3 0.0 copy-done
  75.3 0.0 copy-done.8
  75.3 0.5 convolution_add_fusion
  75.8 3.2 %collective-permute-start = (f32[256,32]{0,1:T(8,128)S(1)}, f32[256,32]{0,1:T(8,128)S(1)}, u32[]{:S(2)}, u32[]{:S(2)}) collective-permute-start(f32[256,32]{0,1:T(8,128)S(1)} %constant_dynamic-slice_fusion), channel_id=1, source_target_pairs={{0,2},{2,0},{1,3},{3,1},{4,6},{6,4},{5,7},{7,5},{8,10},{10,8},{9,1... | collective-permute-start | bytes 98312 | tf_op jit(solution)/shard_map/ppermute | solution.py:21
  80.4 0.0 collective-permute-done
  80.4 0.0 copy-done.4
  80.4 0.6 fusion.25
  (10 shorter events, 0.2 us)
Async XLA Ops:
  7.2 68.1 %copy-start = (bf16[1536,64]{0,1:T(8,128)(2,1)S(1)}, bf16[1536,64]{0,1:T(8,128)(2,1)}, u32[]{:S(2)}) copy-start(bf16[1536,64]{0,1:T(8,128)(2,1)} %param.18) | copy-start | bytes 589828
  7.2 12.1 %copy-start.1 = (bf16[1,1,256,1024]{3,2,1,0:T(8,128)(2,1)S(1)}, bf16[1,1,256,1024]{3,2,1,0:T(8,128)(2,1)}, u32[]{:S(2)}) copy-start(bf16[1,1,256,1024]{3,2,1,0:T(8,128)(2,1)} %param.14) | copy-start | bytes 1572868
  7.2 64.7 %all-gather.2.cloned.1.call-start = ((), (), s32[]{:S(2)}) async-start(), calls=%async_computation.4 | async-start | bytes 3538944 | tf_op jit(solution)/shard_map/all_gather | solution.py:135
  19.9 1.1 %copy-start.2 = (bf16[1,1,256,1024]{3,2,1,0:T(8,128)(2,1)S(1)}, bf16[1,1,256,1024]{3,2,1,0:T(8,128)(2,1)}, u32[]{:S(2)}) copy-start(bf16[1,1,256,1024]{3,2,1,0:T(8,128)(2,1)} %param.13) | copy-start | bytes 1572868
  22.0 19.1 %copy-start.3 = (bf16[1,1,256,1024]{3,2,1,0:T(8,128)(2,1)S(1)}, bf16[1,1,256,1024]{3,2,1,0:T(8,128)(2,1)}, u32[]{:S(2)}) copy-start(bf16[1,1,256,1024]{3,2,1,0:T(8,128)(2,1)} %param.15) | copy-start | bytes 1572868
  37.7 9.7 %all-to-all-start.1 = ((bf16[256,2,512]{2,0,1:T(8,128)(2,1)}), bf16[256,2,512]{2,0,1:T(8,128)(2,1)S(1)}, u32[]{:S(2)}, u32[]{:S(2)}) async-start(bf16[256,2,512]{2,0,1:T(8,128)(2,1)} %get-tuple-element.33), calls=%async_computation.1 | async-start | bytes 1048576 | tf_op jit(solution)/shard_map/all_to_all | solution.py:122
  47.4 9.3 %all-to-all-start.2 = ((bf16[256,2,512]{2,0,1:T(8,128)(2,1)}), bf16[256,2,512]{2,0,1:T(8,128)(2,1)S(1)}, u32[]{:S(2)}, u32[]{:S(2)}) async-start(bf16[256,2,512]{2,0,1:T(8,128)(2,1)} %copy.24), calls=%async_computation.2 | async-start | bytes 1048576 | tf_op jit(solution)/shard_map/all_to_all | solution.py:123
  59.9 5.0 %copy-start.6 = (f32[1,1536]{1,0:T(1,128)S(1)}, f32[1,1536]{1,0:T(1,128)}, u32[]{:S(2)}) copy-start(f32[1,1536]{1,0:T(1,128)} %param.20) | copy-start | bytes 18436
  59.9 5.0 %copy-start.5 = (f32[1,2,1536]{2,1,0:T(2,128)S(1)}, f32[1,2,1536]{2,1,0:T(2,128)}, u32[]{:S(2)}) copy-start(f32[1,2,1536]{2,1,0:T(2,128)} %param.21) | copy-start | bytes 36868
  59.9 12.0 %copy-start.7 = (bf16[1,1,256,1536]{3,2,1,0:T(8,128)(2,1)S(1)}, bf16[1,1,256,1536]{3,2,1,0:T(8,128)(2,1)}, u32[]{:S(2)}) copy-start(bf16[1,1,256,1536]{3,2,1,0:T(8,128)(2,1)} %param.16) | copy-start | bytes 2359300
  61.3 9.3 %all-to-all-start.3 = ((bf16[2,256,512]{2,1,0:T(8,128)(2,1)}), bf16[2,256,512]{2,1,0:T(8,128)(2,1)S(1)}, u32[]{:S(2)}, u32[]{:S(2)}) async-start(bf16[2,256,512]{2,1,0:T(8,128)(2,1)} %all_to_all.53), calls=%async_computation.3 | async-start | bytes 1048576 | tf_op jit(solution)/shard_map/all_to_all | solution.py:132
  71.9 3.3 %copy-start.8 = (f32[64]{0:T(128)S(1)}, f32[64]{0:T(128)}, u32[]{:S(2)}) copy-start(f32[64]{0:T(128)} %param.19) | copy-start | bytes 772
  74.9 5.5 %copy-start.4 = (f32[1,256,32]{1,2,0:T(8,128)S(1)}, f32[1,256,32]{1,2,0:T(8,128)}, u32[]{:S(2)}) copy-start(f32[1,256,32]{1,2,0:T(8,128)} %param.25) | copy-start | bytes 98308
  75.8 4.6 %collective-permute-start = (f32[256,32]{0,1:T(8,128)S(1)}, f32[256,32]{0,1:T(8,128)S(1)}, u32[]{:S(2)}, u32[]{:S(2)}) collective-permute-start(f32[256,32]{0,1:T(8,128)S(1)} %constant_dynamic-slice_fusion), channel_id=1, source_target_pairs={{0,2},{2,0},{1,3},{3,1},{4,6},{6,4},{5,7},{7,5},{8,10},{10,8},{9,1... | collective-permute-start | bytes 98312 | tf_op jit(solution)/shard_map/ppermute | solution.py:21
Sparse Core Ops, SparseCore 0:
  10.2 61.6 all-gather.1
where the time goes:
time: 88.6 us; the launch traced here: 87.9 us
  between operations  22.4 us (25%)
  waiting for transfers between devices  16 us (18%)
  starting transfers between devices  13.7 us (15%)
  local copies, waits for them, and re-layouts  10.5 us (12%)
  blocking collectives  10.2 us (12%)
  other arithmetic  10.1 us (11%)
  matrix products  5.09 us (6%)
    all_to_all x1, blocking collectives, on_device(): lax.all_to_all(rot_q, 'seq', split_axis=1, concat_axis=0, tiled=True)  10.2 us
    all_to_all x1, waiting for transfers between devices, on_device(): lax.all_to_all(head_result, 'seq', split_axis=0, concat_axis=1, tiled=True)  5.72 us
    convert_element_type x1, other arithmetic, rotary(): return turned.astype(jnp.bfloat16)  5.45 us
    all_to_all x1, waiting for transfers between devices, on_device(): lax.all_to_all(rot_k, 'seq', split_axis=1, concat_axis=0, tiled=True)  4.96 us
    convert_element_type x2, local copies, waits for them, and re-layouts, rotary(): source = vectors.astype(jnp.float32)  4.14 us
    all_to_all x1, waiting for transfers between devices, on_device(): lax.all_to_all(values[0, 0], 'seq', split_axis=1, concat_axis=0, tiled=True)  3.57 us
    all_to_all x1, starting transfers between devices, on_device(): lax.all_to_all(rot_k, 'seq', split_axis=1, concat_axis=0, tiled=True)  3.49 us
    all_to_all x1, starting transfers between devices, on_device(): lax.all_to_all(values[0, 0], 'seq', split_axis=1, concat_axis=0, tiled=True)  3.49 us
  transfers between devices with their start and end apart: 5, of which 4 were waited for; matrix products, arithmetic and copies ran while one was open for 22% of the time, Pallas kernels for 0%

commit v1 on v0

--- a/solution.py
+++ b/solution.py
@@ -9,6 +9,18 @@
 masked_score = -1e30
 norm_eps = 1e-06
 shift_factor = 5.0
+
+
+def compute_modes(x0):
+    return jnp.concatenate(
+        lax.all_to_all(
+            jnp.stack(jnp.split(x0, lax.axis_size("seq"), axis=1), axis=0),
+            "seq",
+            split_axis=0,
+            concat_axis=0,
+        ),
+        axis=0,
+    )
 
 
 def partner_2(block, axis, distance):
@@ -118,7 +130,7 @@
     rot_q = rotary(queries[0, 0], grid_dims, first_token)
     rot_k = rotary(key_vectors[0, 0], grid_dims, first_token)
     head_q, head_k, head_v = (
-        lax.all_to_all(rot_q, "seq", split_axis=1, concat_axis=0, tiled=True),
+        compute_modes(rot_q),
         lax.all_to_all(rot_k, "seq", split_axis=1, concat_axis=0, tiled=True),
         lax.all_to_all(values[0, 0], "seq", split_axis=1, concat_axis=0, tiled=True),
     )

time: 88.6 us -> 92.8 us (1.047)
  blocking collectives: 10.2 us -> 0 us
  other arithmetic: 10.1 us -> 17.4 us
  starting transfers between devices: 13.7 us -> 16.9 us
  waiting for transfers between devices: 16 us -> 18.2 us
  local copies, waits for them, and re-layouts: 10.5 us -> 12.2 us
    all_to_all x1 -> x0, blocking collectives: 10.2 us -> none  [on_device(): lax.all_to_all(rot_q, 'seq', split_axis=1, concat_axis=0, tiled=True)]
    convert_element_type x1 -> x2, other arithmetic: 5.45 us -> 11.2 us  [rotary(): return turned.astype(jnp.bfloat16)]
    all_to_all x1, waiting for transfers between devices: 4.96 us -> 0.01 us  [on_device(): lax.all_to_all(rot_k, 'seq', split_axis=1, concat_axis=0, tiled=True)]
    all_to_all x0 -> x1, waiting for transfers between devices: none -> 4.83 us  [compute_modes(): lax.all_to_all(jnp.stack(jnp.split(x0, lax.axis_size('seq'), axis=1), axi...]
    all_to_all x0 -> x1, starting transfers between devices: none -> 3.49 us  [compute_modes(): lax.all_to_all(jnp.stack(jnp.split(x0, lax.axis_size('seq'), axis=1), axi...]
    all_to_all x1, waiting for transfers between devices: 3.57 us -> 6.6 us  [on_device(): lax.all_to_all(values[0, 0], 'seq', split_axis=1, concat_axis=0, tiled=True)]
    all_to_all x2, local copies, waits for them, and re-layouts: 1.24 us -> 4.11 us  [on_device(): lax.all_to_all(values[0, 0], 'seq', split_axis=1, concat_axis=0, tiled=True)]
    convert_element_type x2 -> x1, local copies, waits for them, and re-layouts: 4.14 us -> 2.07 us  [rotary(): source = vectors.astype(jnp.float32)]
  transfers between devices with their start and end apart: 5 -> 6, of which waited for: 4 -> 3; matrix products, arithmetic and copies ran while one was open for 22% -> 29% of each run, Pallas kernels for 0% -> 0%
where the time goes in v1:
time: 92.8 us; the launch traced here: 91.9 us
  between operations  22.2 us (24%)
  waiting for transfers between devices  18.2 us (20%)
  other arithmetic  17.4 us (19%)
  starting transfers between devices  16.9 us (18%)
  local copies, waits for them, and re-layouts  12.2 us (13%)
  matrix products  5.09 us (5%)
    convert_element_type x2, other arithmetic, rotary(): return turned.astype(jnp.bfloat16)  11.2 us
    all_to_all x1, waiting for transfers between devices, on_device(): lax.all_to_all(values[0, 0], 'seq', split_axis=1, concat_axis=0, tiled=True)  6.6 us
    all_to_all x1, waiting for transfers between devices, on_device(): lax.all_to_all(head_result, 'seq', split_axis=0, concat_axis=1, tiled=True)  6.02 us
    all_to_all x1, waiting for transfers between devices, compute_modes(): lax.all_to_all(jnp.stack(jnp.split(x0, lax.axis_size('seq'), axis=1), axi...  4.83 us
    all_to_all x2, local copies, waits for them, and re-layouts, on_device(): lax.all_to_all(values[0, 0], 'seq', split_axis=1, concat_axis=0, tiled=True)  4.11 us
    all_to_all x1, starting transfers between devices, compute_modes(): lax.all_to_all(jnp.stack(jnp.split(x0, lax.axis_size('seq'), axis=1), axi...  3.49 us
    all_to_all x1, starting transfers between devices, on_device(): lax.all_to_all(values[0, 0], 'seq', split_axis=1, concat_axis=0, tiled=True)  3.49 us
    all_to_all x1, starting transfers between devices, on_device(): lax.all_to_all(rot_k, 'seq', split_axis=1, concat_axis=0, tiled=True)  3.49 us
  transfers between devices with their start and end apart: 6, of which 3 were waited for; matrix products, arithmetic and copies ran while one was open for 29% of the time, Pallas kernels for 0%

profile of v1, /device:TPU:1, one launch (start us, length us, event | category | flops | bytes accessed | tf_op | source)
XLA Modules:
  0.0 91.9 jit_solution(11924851170473194500)
XLA Ops:
  7.2 0.0 copy-start
  7.2 0.0 all-gather.2.cloned.1.call-start
  7.2 0.7 all-gather.2.cloned.1.call-update
  7.9 1.4 %fusion.40 = (s32[1,1]{1,0:T(1,128)}, s32[1,1]{1,0:T(1,128)}, s32[1,1]{1,0:T(1,128)}) fusion(s32[1,3]{1,0:T(1,128)} %param.22), kind=kLoop, calls=%fused_computation.94 | loop fusion | bytes 24 | tf_op jit(solution)/shard_map/slice | solution.py:128
  10.6 0.1 and_select_fusion.6
  13.9 2.1 %reshape.244 = f32[256,2,512]{2,1,0:T(2,128)S(1)} reshape(bf16[1,1,256,1024]{3,2,1,0:T(8,128)(2,1)} %param.14) | data formatting | bytes 1572864 | tf_op jit(solution)/shard_map/convert_element_type | solution.py:63
  16.0 0.9 and_select_fusion.3
  17.0 1.2 %convert_bitcast_fusion = f32[256,1024]{1,0:T(8,128)S(1)} fusion(bf16[1,1,256,1024]{3,2,1,0:T(8,128)(2,1)} %param.14), kind=kLoop, calls=%fused_computation.38 | loop fusion | flops 262144 | bytes 1572864 | tf_op jit(solution)/shard_map/convert_element_type | solution.py:63
  18.2 0.1 fusion.39
  18.3 0.4 fusion.38
  18.7 0.4 pad_maximum_fusion
  19.1 0.0 copy-start.1
  19.1 5.2 %fusion.11 = bf16[256,2,512]{2,0,1:T(8,128)(2,1)} fusion(f32[32,2,8,512]{3,2,1,0:T(8,128)S(1)} %bitcast.54, f32[32,2,8,512]{3,2,1,0:T(8,128)S(1)} %bitcast.53, f32[256,2,512]{2,1,0:T(2,128)S(1)} %reshape.244, f32[2,512]{1,0:T(2,128)S(1)} %get-tuple-element.48, f32[2,512]{1,0:T(2,128)S(1)} %get-tuple-element.47, s32[256]{0:T(256)S(1)} %get-tuple-element.43, ...), kind=kLoop, calls=%fused_computation.19 | loop fusion | flops 2621440 | bytes 3684352 | tf_op jit(solution)/shard_map/convert_element_type | solution.py:67
  24.4 3.5 %all-to-all-start.1 = ((bf16[256,2,512]{2,0,1:T(8,128)(2,1)}), bf16[256,2,512]{2,0,1:T(8,128)(2,1)S(1)}, u32[]{:S(2)}, u32[]{:S(2)}) async-start(bf16[256,2,512]{2,0,1:T(8,128)(2,1)} %fusion.11), calls=%async_computation.1 | async-start | bytes 1048576 | tf_op jit(solution)/shard_map/all_to_all | solution.py:134
  27.9 0.0 copy-done.1
  27.9 0.1 bitcast_convert_fusion
  28.0 0.7 fusion.36
  28.7 0.4 fusion.37
  29.2 2.2 %all_to_all.42 = bf16[256,2,512]{2,1,0:T(2,128)(2,1)} reshape(bf16[1,1,256,1024]{3,2,1,0:T(8,128)(2,1)} %param.15) | data formatting | bytes 1048576 | tf_op jit(solution)/shard_map/all_to_all | solution.py:135
  31.4 1.9 %copy.21 = bf16[256,2,512]{2,0,1:T(8,128)(2,1)} copy(bf16[256,2,512]{2,1,0:T(2,128)(2,1)} %all_to_all.42) | data formatting | bytes 1048576 | tf_op jit(solution)/shard_map/all_to_all | solution.py:135
  33.3 6.0 %fusion.14 = bf16[256,1024]{1,0:T(8,128)(2,1)} fusion(f32[256,1]{1,0:T(8,128)} %get-tuple-element.17, f32[256,1023]{1,0:T(8,128)S(1)} %get-tuple-element.25, f32[256,1023]{1,0:T(8,128)S(1)} %get-tuple-element.24, f32[256,1]{1,0:T(8,128)S(1)} %get-tuple-element.16, f32[1024]{0:T(1024)S(1)} %get-tuple-element.52, f32[1024]{0:T(1024)S(1)} %get-tuple-element.51, ...), kind=kLoop, calls=%fused_computation.23 | loop fusion | flops 3407872 | bytes 3160064 | tf_op jit(solution)/shard_map/convert_element_type | solution.py:67
  39.3 0.0 all-to-all-done.1
  39.3 3.5 %all-to-all-start.2 = ((bf16[256,2,512]{2,0,1:T(8,128)(2,1)}), bf16[256,2,512]{2,0,1:T(8,128)(2,1)S(1)}, u32[]{:S(2)}, u32[]{:S(2)}) async-start(bf16[256,2,512]{2,0,1:T(8,128)(2,1)} %copy.21), calls=%async_computation.2 | async-start | bytes 1048576 | tf_op jit(solution)/shard_map/all_to_all | solution.py:135
  42.8 1.1 %slice_bitcast_fusion.1 = (bf16[1,256,512]{2,1,0:T(8,128)(2,1)S(1)}, bf16[1,256,512]{2,1,0:T(8,128)(2,1)S(1)}) fusion(bf16[256,1024]{1,0:T(8,128)(2,1)} %fusion.14), kind=kLoop, calls=%fused_computation.37 | loop fusion | bytes 1048576 | tf_op jit(solution)/shard_map/stack | solution.py:17
  43.8 0.9 pad_maximum_fusion.2
  44.7 6.6 %all-to-all-done.2 = bf16[256,2,512]{2,0,1:T(8,128)(2,1)S(1)} async-done(((bf16[256,2,512]{2,0,1:T(8,128)(2,1)}), bf16[256,2,512]{2,0,1:T(8,128)(2,1)S(1)}, u32[]{:S(2)}, u32[]{:S(2)}) %all-to-all-start.2) | async-done | bytes 524320 | tf_op jit(solution)/shard_map/all_to_all | solution.py:135
  51.3 3.5 %all-to-all-start = ((bf16[2,256,512]{2,1,0:T(8,128)(2,1)}), bf16[2,256,512]{2,1,0:T(8,128)(2,1)S(1)}, u32[]{:S(2)}, u32[]{:S(2)}) async-start(bf16[2,256,512]{2,1,0:T(8,128)(2,1)} %pad_maximum_fusion.2), calls=%async_computation | async-start | bytes 1048576 | tf_op jit(solution)/shard_map/all_to_all | solution.py:16
  56.7 0.1 reshape.234
  56.9 0.1 reshape.235
  57.0 4.8 %all-to-all-done = bf16[2,256,512]{2,1,0:T(8,128)(2,1)S(1)} async-done(((bf16[2,256,512]{2,1,0:T(8,128)(2,1)}), bf16[2,256,512]{2,1,0:T(8,128)(2,1)S(1)}, u32[]{:S(2)}, u32[]{:S(2)}) %all-to-all-start) | async-done | bytes 524320 | tf_op jit(solution)/shard_map/all_to_all | solution.py:16
  61.8 0.1 reshape_reshape.3
  62.0 0.7 fusion.19
  62.7 1.4 %fusion.41 = (f32[4,512]{1,0:T(4,128)S(1)}, f32[4,512,512]{1,2,0:T(8,128)S(1)}) fusion(f32[4,512,512]{1,2,0:T(8,128)S(1)} %fusion.19, pred[512]{0:T(512)(128)(4,1)S(1)} %iota_compare_fusion), kind=kOutput, calls=%fused_computation.95 | output fusion | flops 6291967 | bytes 8397312 | tf_op jit(solution)/shard_map/while/body/eval_jaxpr/sub | solution.py:99
  64.1 0.9 fusion.8
  65.0 0.0 copy-start.4
  65.0 0.0 copy-start.3
  65.0 0.0 copy-start.5
  65.1 0.4 copy.24
  65.5 1.0 %all_to_all.45 = bf16[2,256,512]{2,1,0:T(8,128)(2,1)} reshape(bf16[512,4,128]{2,1,0:T(4,128)(2,1)S(1)} %copy.24) | data formatting | bytes 1048576 | tf_op jit(solution)/shard_map/all_to_all | solution.py:144
  66.5 3.5 %all-to-all-start.3 = ((bf16[2,256,512]{2,1,0:T(8,128)(2,1)}), bf16[2,256,512]{2,1,0:T(8,128)(2,1)S(1)}, u32[]{:S(2)}, u32[]{:S(2)}) async-start(bf16[2,256,512]{2,1,0:T(8,128)(2,1)} %all_to_all.45), calls=%async_computation.3 | async-start | bytes 1048576 | tf_op jit(solution)/shard_map/all_to_all | solution.py:144
  70.0 0.0 copy-done.4
  70.0 0.0 copy-done.3
  70.1 6.0 %all-to-all-done.3 = bf16[2,256,512]{2,1,0:T(8,128)(2,1)S(1)} async-done(((bf16[2,256,512]{2,1,0:T(8,128)(2,1)}), bf16[2,256,512]{2,1,0:T(8,128)(2,1)S(1)}, u32[]{:S(2)}, u32[]{:S(2)}) %all-to-all-start.3) | async-done | bytes 524320 | tf_op jit(solution)/shard_map/all_to_all | solution.py:144
  76.1 0.2 copy.25
  76.3 0.0 all-gather.2.cloned.1.call-done
  76.3 0.0 copy-done.5
  76.3 0.0 copy-start.6
  76.3 3.0 %fusion.42 = (f32[256]{0:T(256)S(1)}, f32[256,1536]{1,0:T(8,128)S(1)}) fusion(bf16[256,1024]{0,1:T(8,128)(2,1)S(1)} %bitcast.58, bf16[1024,1536]{1,0:T(8,128)(2,1)} %all-gather.2.cloned.1.call-done, f32[1536]{0:T(1024)S(1)} %reduce, bf16[1,1,256,1536]{3,2,1,0:T(8,128)(2,1)S(1)} %copy-done.5), kind=kOutput, calls=%fused_computation.96 | convolution fusion | flops 806878976 | bytes 6036480 | tf_op jit(solution)/shard_map/dot_general | solution.py:145
  79.3 0.0 copy-start.2
  79.3 0.3 multiply_reduce_fusion
  79.7 0.0 copy-done
  79.7 0.0 copy-done.6
  79.7 0.5 convolution_add_fusion
  80.2 2.9 %collective-permute-start = (f32[256,32]{0,1:T(8,128)S(1)}, f32[256,32]{0,1:T(8,128)S(1)}, u32[]{:S(2)}, u32[]{:S(2)}) collective-permute-start(f32[256,32]{0,1:T(8,128)S(1)} %constant_dynamic-slice_fusion), channel_id=1, source_target_pairs={{0,2},{2,0},{1,3},{3,1},{4,6},{6,4},{5,7},{7,5},{8,10},{10,8},{9,1... | collective-permute-start | bytes 98312 | tf_op jit(solution)/shard_map/ppermute | solution.py:33
  84.4 0.0 collective-permute-done
  84.4 0.0 copy-done.2
  84.5 0.6 fusion.31
  (13 shorter events, 0.2 us)
Async XLA Ops:
  7.2 72.5 %copy-start = (bf16[1536,64]{0,1:T(8,128)(2,1)S(1)}, bf16[1536,64]{0,1:T(8,128)(2,1)}, u32[]{:S(2)}) copy-start(bf16[1536,64]{0,1:T(8,128)(2,1)} %param.18) | copy-start | bytes 589828
  7.2 69.1 %all-gather.2.cloned.1.call-start = ((), (), s32[]{:S(2)}) async-start(), calls=%async_computation.4 | async-start | bytes 3538944 | tf_op jit(solution)/shard_map/all_gather | solution.py:147
  19.1 8.8 %copy-start.1 = (bf16[1,1,256,1024]{3,2,1,0:T(8,128)(2,1)S(1)}, bf16[1,1,256,1024]{3,2,1,0:T(8,128)(2,1)}, u32[]{:S(2)}) copy-start(bf16[1,1,256,1024]{3,2,1,0:T(8,128)(2,1)} %param.13) | copy-start | bytes 1572868
  24.4 14.9 %all-to-all-start.1 = ((bf16[256,2,512]{2,0,1:T(8,128)(2,1)}), bf16[256,2,512]{2,0,1:T(8,128)(2,1)S(1)}, u32[]{:S(2)}, u32[]{:S(2)}) async-start(bf16[256,2,512]{2,0,1:T(8,128)(2,1)} %fusion.11), calls=%async_computation.1 | async-start | bytes 1048576 | tf_op jit(solution)/shard_map/all_to_all | solution.py:134
  39.3 12.0 %all-to-all-start.2 = ((bf16[256,2,512]{2,0,1:T(8,128)(2,1)}), bf16[256,2,512]{2,0,1:T(8,128)(2,1)S(1)}, u32[]{:S(2)}, u32[]{:S(2)}) async-start(bf16[256,2,512]{2,0,1:T(8,128)(2,1)} %copy.21), calls=%async_computation.2 | async-start | bytes 1048576 | tf_op jit(solution)/shard_map/all_to_all | solution.py:135
  51.3 10.5 %all-to-all-start = ((bf16[2,256,512]{2,1,0:T(8,128)(2,1)}), bf16[2,256,512]{2,1,0:T(8,128)(2,1)S(1)}, u32[]{:S(2)}, u32[]{:S(2)}) async-start(bf16[2,256,512]{2,1,0:T(8,128)(2,1)} %pad_maximum_fusion.2), calls=%async_computation | async-start | bytes 1048576 | tf_op jit(solution)/shard_map/all_to_all | solution.py:16
  65.0 5.0 %copy-start.4 = (f32[1,1536]{1,0:T(1,128)S(1)}, f32[1,1536]{1,0:T(1,128)}, u32[]{:S(2)}) copy-start(f32[1,1536]{1,0:T(1,128)} %param.20) | copy-start | bytes 18436
  65.0 5.0 %copy-start.3 = (f32[1,2,1536]{2,1,0:T(2,128)S(1)}, f32[1,2,1536]{2,1,0:T(2,128)}, u32[]{:S(2)}) copy-start(f32[1,2,1536]{2,1,0:T(2,128)} %param.21) | copy-start | bytes 36868
  65.0 11.3 %copy-start.5 = (bf16[1,1,256,1536]{3,2,1,0:T(8,128)(2,1)S(1)}, bf16[1,1,256,1536]{3,2,1,0:T(8,128)(2,1)}, u32[]{:S(2)}) copy-start(bf16[1,1,256,1536]{3,2,1,0:T(8,128)(2,1)} %param.16) | copy-start | bytes 2359300
  66.5 9.6 %all-to-all-start.3 = ((bf16[2,256,512]{2,1,0:T(8,128)(2,1)}), bf16[2,256,512]{2,1,0:T(8,128)(2,1)S(1)}, u32[]{:S(2)}, u32[]{:S(2)}) async-start(bf16[2,256,512]{2,1,0:T(8,128)(2,1)} %all_to_all.45), calls=%async_computation.3 | async-start | bytes 1048576 | tf_op jit(solution)/shard_map/all_to_all | solution.py:144
  76.3 3.3 %copy-start.6 = (f32[64]{0:T(128)S(1)}, f32[64]{0:T(128)}, u32[]{:S(2)}) copy-start(f32[64]{0:T(128)} %param.19) | copy-start | bytes 772
  79.3 5.1 %copy-start.2 = (f32[1,256,32]{1,2,0:T(8,128)S(1)}, f32[1,256,32]{1,2,0:T(8,128)}, u32[]{:S(2)}) copy-start(f32[1,256,32]{1,2,0:T(8,128)} %param.25) | copy-start | bytes 98308
  80.2 4.3 %collective-permute-start = (f32[256,32]{0,1:T(8,128)S(1)}, f32[256,32]{0,1:T(8,128)S(1)}, u32[]{:S(2)}, u32[]{:S(2)}) collective-permute-start(f32[256,32]{0,1:T(8,128)S(1)} %constant_dynamic-slice_fusion), channel_id=1, source_target_pairs={{0,2},{2,0},{1,3},{3,1},{4,6},{6,4},{5,7},{7,5},{8,10},{10,8},{9,1... | collective-permute-start | bytes 98312 | tf_op jit(solution)/shard_map/ppermute | solution.py:33
Sparse Core Ops, SparseCore 0:
  10.2 61.6 all-gather.1
